TPU v7x, 512 devices: a whole 4x4x16 slice. The times are simulated.
512 devices in a mesh: flux: 16 (over z), obs: 32 (over y, x, core).
Axes of the slice: x: 4, y: 4, z: 16, core: 2. Of those that a mesh axis runs over, the one named last changes fastest.
Arguments:
- footprint: bfloat16 [4096, 4, 4, 2, 4096], P(('flux', 'obs')), may hold values from 0.00049972534 to 0.049804688
- obs_hour: int32 [4096, 4], P(('flux', 'obs')), may hold values from 0 to 3
- tile_list: int32 [4096, 4], P(('flux', 'obs')), may hold values from 0 to 511, as said below
- tile_row: int32 [512], replicated, may hold values from 0 to 511, as said below
- flux: bfloat16 [512, 5, 4096], P('flux'), may hold values from -6 to 6
- observed: float32 [4096, 4], P(('flux', 'obs')), may hold values from -18 to 18
- obs_var: float32 [4096, 4], P(('flux', 'obs')), may hold values from 0.5 to 4
Outputs:
- modeled: float32 [4096, 4], P(('flux', 'obs'))
- gradient: float32 [512, 5, 4096], P('flux', None, 'obs')
Inputs may be any that keep to these rules, and one draw needn't show every extreme that they name: `tile_row`: A permutation: every tile has its own storage row, and the row r lies on index r // 32 of flux. `tile_list`: among the 32 listed tiles of one device's 8 blocks, at most 4 have storage rows on one index of flux; on every device some index of flux gets exactly 4.
All inputs are finite; a program needn't handle non-finite values.
Results may differ from a plain program's by a relative error of at most 0.0019.
Values may be sent and summed in bfloat16 or wider, within the bound.
A program may use at most 64 MiB of HBM per device.

v0:
```python
import jax
import jax.numpy as jnp
from jax import lax
from jax.sharding import PartitionSpec as P


def shards(footprint, obs_hour, tile_list, tile_row, flux, observed, obs_var):
    columns = lax.axis_size("obs")
    block_count, slot_width, sounding_count, lag_count, cell_count = footprint.shape
    tile_count, hour_count, _ = flux.shape
    chunk = cell_count // columns
    me = lax.axis_index("obs")
    table_hits = tile_list[..., None] == jnp.arange(tile_row.shape[0], dtype=jnp.int32)
    storage = jnp.sum(jnp.where(table_hits, tile_row, 0), axis=-1)
    numbers = jnp.concatenate(
        [storage.astype(jnp.float32), obs_hour.astype(jnp.float32), observed, obs_var], axis=1
    )
    numbers = lax.all_gather(numbers, "obs", axis=0, tiled=True)
    rows = numbers[:, 0:4].astype(jnp.int32)
    hours = numbers[:, 4:8].astype(jnp.int32)
    own_flux = lax.dynamic_slice_in_dim(flux, me * chunk, chunk, axis=2)
    all_flux = lax.all_gather(own_flux, "flux", axis=0, tiled=True)
    total = all_flux.shape[0]
    feet = footprint.reshape(-1, columns, chunk).transpose(1, 0, 2)
    feet = lax.all_to_all(feet, "obs", split_axis=0, concat_axis=0, tiled=True)
    blocks = block_count * columns
    feet = feet.reshape(blocks, slot_width, sounding_count, lag_count, chunk)
    onehot = rows.reshape(-1)[:, None] == jnp.arange(total, dtype=jnp.int32)[None, :]
    windows = jnp.dot(
        onehot.astype(jnp.bfloat16),
        all_flux.reshape(total, hour_count * chunk),
        preferred_element_type=jnp.float32,
    ).reshape(blocks, slot_width, hour_count, chunk)
    hour_at = hours[:, :, None] + jnp.arange(lag_count, dtype=jnp.int32)
    select = hour_at[..., None] == jnp.arange(hour_count, dtype=jnp.int32)
    picked = 0.0
    for h in range(hour_count):
        picked = picked + jnp.where(
            select[:, None, :, :, h, None], windows[:, :, None, None, h, :], 0.0
        )
    partial_value = jnp.sum(feet.astype(jnp.float32) * picked, axis=(1, 3, 4))
    modeled_all = lax.psum(partial_value, "obs")
    scaled = ((modeled_all - numbers[:, 8:12]) / numbers[:, 12:16]).astype(jnp.bfloat16)
    modeled = lax.dynamic_slice_in_dim(modeled_all, me * block_count, block_count, axis=0)
    coefficient = jnp.where(select, scaled.astype(jnp.float32)[:, :, None, None], 0.0)
    terms = []
    for h in range(hour_count):
        terms.append(
            jnp.sum(feet.astype(jnp.float32) * coefficient[:, None, :, :, h, None], axis=(2, 3))
        )
    terms = jnp.stack(terms, axis=2).reshape(blocks * slot_width, hour_count * chunk)
    high = terms.astype(jnp.bfloat16)
    low = (terms - high.astype(jnp.float32)).astype(jnp.bfloat16)
    spread = onehot.astype(jnp.bfloat16)
    summed = lax.dot_general(
        spread, high, (((0,), (0,)), ((), ())), preferred_element_type=jnp.float32
    ) + lax.dot_general(spread, low, (((0,), (0,)), ((), ())), preferred_element_type=jnp.float32)
    gradient = lax.psum_scatter(
        summed.reshape(total, hour_count, chunk), "flux", scatter_dimension=0, tiled=True
    )
    return (modeled, gradient)


def solution(mesh):
    placed = (
        P(("flux", "obs"), None, None, None, None),
        P(("flux", "obs"), None),
        P(("flux", "obs"), None),
        P(),
        P("flux", None, None),
        P(("flux", "obs"), None),
        P(("flux", "obs"), None),
    )
    return jax.shard_map(
        shards,
        mesh=mesh,
        in_specs=placed,
        out_specs=(P(("flux", "obs"), None), P("flux", None, "obs")),
        check_vma=False,
    )
```

profile of v0, /device:TPU:8, one launch (start us, length us, event | category | flops | bytes accessed | tf_op | source)
XLA Modules:
  0.0 355.8 jit_solution(15153389452616925642)
XLA Ops:
  7.2 3.4 reshape.75
  10.7 2.2 copy.126
  12.8 9.5 %all-to-all-start = ((bf16[32,256,128]{2,1,0:T(8,128)(2,1)}), bf16[32,256,128]{2,1,0:T(8,128)(2,1)S(1)}, u32[]{:S(2)}, u32[]{:S(2)}) async-start(bf16[32,256,128]{2,1,0:T(8,128)(2,1)} %copy.126), calls=%async_computation | async-start | bytes 4194304 | tf_op jit(solution)/shard_map/all_to_all | solution.py:25
  22.8 42.4 %all_gather.6 = f32[256,16]{1,0:T(8,128)S(1)} all-gather(f32[8,16]{1,0:T(8,128)S(1)} %copy.127), channel_id=1, replica_groups=mesh['flux'=16,'obs'=32] {'obs'}, dimensions={0}, use_global_device_ids=true | all-gather | bytes 16896 | tf_op jit(solution)/shard_map/all_gather | solution.py:18
  67.5 1.6 copy.157
  70.1 1.6 copy.158
  73.2 1.6 copy.139
  74.8 1.6 copy.137
  78.3 2.0 broadcast_in_dim.153
  80.3 2.6 broadcast_in_dim.154
  82.9 2.0 broadcast_in_dim.160
  85.0 3.2 broadcast_in_dim.161
  88.2 2.0 broadcast_in_dim.167
  90.2 3.2 broadcast_in_dim.168
  93.5 2.0 broadcast_in_dim.174
  95.5 3.2 broadcast_in_dim.175
  99.9 2.6 broadcast_in_dim.146
  102.5 39.7 %all_gather.7 = bf16[512,5,128]{2,0,1:T(8,128)(2,1)} all-gather(bf16[32,5,128]{2,0,1:T(8,128)(2,1)S(1)} %constant_dynamic-slice_fusion), channel_id=1, replica_groups=mesh['flux'=16,'obs'=32] {'flux'}, dimensions={0}, use_global_device_ids=true | all-gather | bytes 696320 | tf_op jit(solution)/shard_map/all_gather | solution.py:22
  142.3 2.2 copy.131
  144.4 2.2 fusion.4
  152.5 2.2 broadcast_in_dim.157
  159.2 8.6 %multiply_reduce_fusion.5 = f32[32,256]{1,0:T(8,128)S(1)} fusion(f32[32,256,128]{2,1,0:T(8,128)S(1)} %bitcast.76, f32[32,256,128]{2,1,0:T(8,128)S(1)} %bitcast.75, f32[32,256,128]{2,1,0:T(8,128)S(1)} %bitcast.74, f32[32,256,128]{2,1,0:T(8,128)S(1)} %bitcast.73, f32[32,256,128]{2,1,0:T(8,128)S(1)} %bitcast.77, pred[32,256]{1,0:T(8,128)(4,1)S(1)} %copy-done.7, ...), kind=kLoop, calls=%fused_computation.5 | loop fusion | flops 12574720 | bytes 23142400 | tf_op jit(solution)/shard_map/reduce_sum | solution.py:41
  167.8 4.0 %reduce_sum.72 = f32[256,4,4,2]{3,2,1,0:T(4,128)} reshape(f32[32,256]{1,0:T(8,128)S(1)} %multiply_reduce_fusion.5) | data formatting | bytes 65536 | tf_op jit(solution)/shard_map/reduce_sum | solution.py:41
  171.9 2.1 reduce_sum.73
  174.0 53.2 %psum.7 = f32[256,4]{0,1:T(4,128)S(1)} all-reduce(f32[256,4]{0,1:T(4,128)S(1)} %copy.143), channel_id=1, replica_groups=mesh['flux'=16,'obs'=32] {'obs'}, use_global_device_ids=true, to_apply=%region_3.4 | all-reduce | flops 1024 | bytes 8192 | tf_op jit(solution)/shard_map/psum | solution.py:42
  233.2 18.6 %multiply_reduce_fusion = (f32[256,4,128]{2,1,0:T(4,128)}, f32[256,4,128]{2,1,0:T(4,128)}, f32[256,4,128]{2,1,0:T(4,128)}, f32[256,4,128]{2,1,0:T(4,128)}, f32[256,4,128]{2,1,0:T(4,128)}) fusion(f32[256,4,2]{2,1,0:T(4,128)} %copy.150, f32[256,4,2]{2,1,0:T(4,128)} %copy.149, f32[256,4,2]{2,1,0:T(4,128)} %copy.148, f32[256,4,2]{2,1,0:T(4,128)} %copy.147, ...), kind=kLoop, calls=%fused_computation | loop fusion | flops 10878976 | bytes 4759552 | tf_op jit(solution)/shard_map/reduce_sum | solution.py:49
  251.8 10.5 %stack.23 = f32[256,4,5,128]{3,2,1,0:T(8,128)} concatenate(f32[256,4,1,128]{3,2,1,0:T(1,128)} %bitcast.86, f32[256,4,1,128]{3,2,1,0:T(1,128)} %bitcast.85, f32[256,4,1,128]{3,2,1,0:T(1,128)} %bitcast.84, f32[256,4,1,128]{3,2,1,0:T(1,128)} %bitcast.83, f32[256,4,1,128]{3,2,1,0:T(1,128)} %bitcast.82), dimensions={2} | concatenate | bytes 5242880 | tf_op jit(solution)/shard_map/stack | solution.py:51
  262.3 3.5 fusion.1
  265.8 4.4 %fusion.6 = f32[512,640]{1,0:T(8,128)} fusion(f32[512,640]{1,0:T(8,128)S(1)} %fusion.1, f32[128,8,5,128]{3,2,1,0:T(8,128)} %bitcast.81, s32[1024]{0:T(1024)S(1)} %copy-done.9), kind=kOutput, calls=%fused_computation.15 | convolution fusion | flops 671940608 | bytes 5246976 | tf_op jit(solution)/shard_map/dot_general | solution.py:55
  270.2 1.7 copy.151
  271.9 1.8 copy.152
  274.4 72.9 %reduce-scatter.2.cloned.1.call-done = f32[32,5,128]{2,1,0:T(8,128)} async-done(((f32[512,5,128]{2,1,0:T(8,128)}), f32[32,5,128]{2,1,0:T(8,128)}) %reduce-scatter.2.cloned.1.call-update) | async-done | bytes 81936 | tf_op jit(solution)/shard_map/reduce_scatter | solution.py:58
  (72 shorter events, 26.7 us)
Async XLA Ops:
  7.2 95.3 %copy-start = (bf16[32,5,4096]{2,0,1:T(8,128)(2,1)S(1)}, bf16[32,5,4096]{2,0,1:T(8,128)(2,1)}, u32[]{:S(2)}) copy-start(bf16[32,5,4096]{2,0,1:T(8,128)(2,1)} %param.11) | copy-start | bytes 3932164
  10.6 11.8 %copy-start.12 = (s32[8,4]{0,1:T(4,128)S(1)}, s32[8,4]{0,1:T(4,128)}, u32[]{:S(2)}) copy-start(s32[8,4]{0,1:T(4,128)} %param.8) | copy-start | bytes 388
  10.6 11.8 %copy-start.10 = (s32[512]{0:T(512)S(1)}, s32[512]{0:T(512)}, u32[]{:S(2)}) copy-start(s32[512]{0:T(512)} %param.10) | copy-start | bytes 6148
  10.6 11.8 %copy-start.11 = (s32[8,4]{0,1:T(4,128)S(1)}, s32[8,4]{0,1:T(4,128)}, u32[]{:S(2)}) copy-start(s32[8,4]{0,1:T(4,128)} %param.9) | copy-start | bytes 388
  10.7 12.1 %copy-start.13 = (f32[8,4]{0,1:T(4,128)S(1)}, f32[8,4]{0,1:T(4,128)}, u32[]{:S(2)}) copy-start(f32[8,4]{0,1:T(4,128)} %param.13) | copy-start | bytes 388
  10.7 12.1 %copy-start.14 = (f32[8,4]{0,1:T(4,128)S(1)}, f32[8,4]{0,1:T(4,128)}, u32[]{:S(2)}) copy-start(f32[8,4]{0,1:T(4,128)} %param.12) | copy-start | bytes 388
  12.8 139.7 %all-to-all-start = ((bf16[32,256,128]{2,1,0:T(8,128)(2,1)}), bf16[32,256,128]{2,1,0:T(8,128)(2,1)S(1)}, u32[]{:S(2)}, u32[]{:S(2)}) async-start(bf16[32,256,128]{2,1,0:T(8,128)(2,1)} %copy.126), calls=%async_computation | async-start | bytes 4194304 | tf_op jit(solution)/shard_map/all_to_all | solution.py:25
  22.4 325.0 %reduce-scatter.2.cloned.1.call-start = ((), (), s32[]{:S(2)}) async-start(), calls=%async_computation.2 | async-start | bytes 2228224 | tf_op jit(solution)/shard_map/reduce_scatter | solution.py:58
  152.5 2.2 copy-start.4
  152.5 3.3 copy-start.3
  154.8 2.2 copy-start.2
  155.9 2.2 copy-start.1
  157.0 2.2 copy-start.5
  157.0 2.2 copy-start.6
  157.0 2.2 copy-start.7
  167.8 59.4 %copy-start.8 = (f32[256,4]{0,1:T(4,128)S(1)}, f32[256,4]{0,1:T(4,128)}, u32[]{:S(2)}) copy-start(f32[256,4]{0,1:T(4,128)} %copy.157) | copy-start | bytes 12292
  251.8 10.5 %copy-start.9 = (s32[1024]{0:T(1024)S(1)}, s32[1024]{0:T(1024)}, u32[]{:S(2)}) copy-start(s32[1024]{0:T(1024)} %eq.73) | copy-start | bytes 12292
Sparse Core Ops, SparseCore 0:
  273.9 73.4 reduce-scatter.1
where the time goes:
time: 358 us; the launch traced here: 356 us
  blocking collectives  135 us (38%)
  local copies, waits for them, and re-layouts  82.3 us (23%)
  waiting for transfers between devices  72.9 us (20%)
  other arithmetic  31.1 us (9%)
  between operations  14.4 us (4%)
  matrix products  10.1 us (3%)
  starting transfers between devices  9.58 us (3%)
    reduce_scatter x1, waiting for transfers between devices, shards(): lax.psum_scatter(summed.reshape(total, hour_count, chunk), 'flux', scatte...  72.9 us
    psum x1, blocking collectives, shards(): modeled_all = lax.psum(partial_value, 'obs')  53.2 us
    broadcast_in_dim x27, local copies, waits for them, and re-layouts, shards(): jnp.where(select[:, None, :, :, h, None], windows[:, :, None, None, h, :]...  43.3 us
    all_gather x1, blocking collectives, shards(): numbers = lax.all_gather(numbers, 'obs', axis=0, tiled=True)  42.4 us
    all_gather x1, blocking collectives, shards(): all_flux = lax.all_gather(own_flux, 'flux', axis=0, tiled=True)  39.7 us
    reduce_sum x1, other arithmetic, shards(): jnp.sum(feet.astype(jnp.float32) * coefficient[:, None, :, :, h, None], a...  18.6 us
    reduce_sum x2, other arithmetic, shards(): partial_value = jnp.sum(feet.astype(jnp.float32) * picked, axis=(1, 3, 4))  10.7 us
    another operation x1, local copies, waits for them, and re-layouts, shards(): jnp.stack(terms, axis=2).reshape(blocks * slot_width, hour_count * chunk)  10.5 us
  transfers between devices with their start and end apart: 2, of which 1 were waited for; matrix products, arithmetic and copies ran while one was open for 14% of the time, Pallas kernels for 0%

commit v1 on v0

--- a/solution.py
+++ b/solution.py
@@ -39,7 +39,7 @@
             select[:, None, :, :, h, None], windows[:, :, None, None, h, :], 0.0
         )
     partial_value = jnp.sum(feet.astype(jnp.float32) * picked, axis=(1, 3, 4))
-    modeled_all = lax.psum(partial_value, "obs")
+    modeled_all = lax.all_gather(partial_value, axis_name="obs").sum(axis=0)
     scaled = ((modeled_all - numbers[:, 8:12]) / numbers[:, 12:16]).astype(jnp.bfloat16)
     modeled = lax.dynamic_slice_in_dim(modeled_all, me * block_count, block_count, axis=0)
     coefficient = jnp.where(select, scaled.astype(jnp.float32)[:, :, None, None], 0.0)

time: 358 us -> 322 us (0.90)
  blocking collectives: 135 us -> 104 us
  waiting for transfers between devices: 72.9 us -> 67.8 us
    psum x1 -> x0, blocking collectives: 53.2 us -> none  [shards(): modeled_all = lax.psum(partial_value, 'obs')]
    all_gather x0 -> x1, blocking collectives: none -> 22.4 us  [shards(): modeled_all = lax.all_gather(partial_value, axis_name='obs').sum(axis=0)]
    reduce_scatter x1, waiting for transfers between devices: 72.9 us -> 67.7 us  [shards(): lax.psum_scatter(summed.reshape(total, hour_count, chunk), 'flux', scatte...]
  transfers between devices with their start and end apart: 2 -> 2, of which waited for: 1 -> 1; matrix products, arithmetic and copies ran while one was open for 14% -> 15% of each run, Pallas kernels for 0% -> 0%
where the time goes in v1:
time: 322 us; the launch traced here: 320 us
  blocking collectives  104 us (32%)
  local copies, waits for them, and re-layouts  82.3 us (26%)
  waiting for transfers between devices  67.8 us (21%)
  other arithmetic  31.2 us (10%)
  between operations  14.4 us (4%)
  matrix products  10.1 us (3%)
  starting transfers between devices  9.58 us (3%)
    reduce_scatter x1, waiting for transfers between devices, shards(): lax.psum_scatter(summed.reshape(total, hour_count, chunk), 'flux', scatte...  67.7 us
    broadcast_in_dim x27, local copies, waits for them, and re-layouts, shards(): jnp.where(select[:, None, :, :, h, None], windows[:, :, None, None, h, :]...  43.3 us
    all_gather x1, blocking collectives, shards(): numbers = lax.all_gather(numbers, 'obs', axis=0, tiled=True)  42.4 us
    all_gather x1, blocking collectives, shards(): all_flux = lax.all_gather(own_flux, 'flux', axis=0, tiled=True)  39.7 us
    all_gather x1, blocking collectives, shards(): modeled_all = lax.all_gather(partial_value, axis_name='obs').sum(axis=0)  22.4 us
    reduce_sum x1, other arithmetic, shards(): jnp.sum(feet.astype(jnp.float32) * coefficient[:, None, :, :, h, None], a...  18.6 us
    reduce_sum x2, other arithmetic, shards(): partial_value = jnp.sum(feet.astype(jnp.float32) * picked, axis=(1, 3, 4))  10.7 us
    another operation x1, local copies, waits for them, and re-layouts, shards(): jnp.stack(terms, axis=2).reshape(blocks * slot_width, hour_count * chunk)  10.5 us
  transfers between devices with their start and end apart: 2, of which 1 were waited for; matrix products, arithmetic and copies ran while one was open for 15% of the time, Pallas kernels for 0%

profile of v1, /device:TPU:8, one launch (start us, length us, event | category | flops | bytes accessed | tf_op | source)
XLA Modules:
  0.0 319.8 jit_solution(13367567219976026790)
XLA Ops:
  7.2 3.4 %reshape.75 = bf16[256,32,128]{2,1,0:T(8,128)(2,1)S(1)} reshape(bf16[8,4,4,2,4096]{4,3,2,1,0:T(2,128)(2,1)} %param.7) | data formatting | bytes 4194304 | tf_op jit(solution)/shard_map/reshape | solution.py:24
  10.7 2.2 copy.154
  12.8 9.5 %all-to-all-start = ((bf16[32,256,128]{2,1,0:T(8,128)(2,1)}), bf16[32,256,128]{2,1,0:T(8,128)(2,1)S(1)}, u32[]{:S(2)}, u32[]{:S(2)}) async-start(bf16[32,256,128]{2,1,0:T(8,128)(2,1)} %copy.154), calls=%async_computation | async-start | bytes 4194304 | tf_op jit(solution)/shard_map/all_to_all | solution.py:25
  22.8 42.4 %all_gather.12 = f32[256,16]{1,0:T(8,128)S(1)} all-gather(f32[8,16]{1,0:T(8,128)S(1)} %copy.155), channel_id=1, replica_groups=mesh['flux'=16,'obs'=32] {'obs'}, dimensions={0}, use_global_device_ids=true | all-gather | bytes 16896 | tf_op jit(solution)/shard_map/all_gather | solution.py:18
  67.5 1.6 copy.185
  70.1 1.6 copy.186
  73.2 1.6 copy.167
  74.8 1.6 copy.165
  78.3 2.0 broadcast_in_dim.153
  80.3 2.6 broadcast_in_dim.154
  82.9 2.0 broadcast_in_dim.160
  85.0 3.2 %broadcast_in_dim.161 = pred[32,256]{1,0:T(8,128)(4,1)} reshape(pred[256,4,4,2]{3,2,1,0:T(4,128)(4,1)} %broadcast_in_dim.160) | data formatting | bytes 16384 | tf_op jit(solution)/shard_map/jit(_where)/broadcast_in_dim | solution.py:38
  88.2 2.0 broadcast_in_dim.167
  90.2 3.2 %broadcast_in_dim.168 = pred[32,256]{1,0:T(8,128)(4,1)} reshape(pred[256,4,4,2]{3,2,1,0:T(4,128)(4,1)} %broadcast_in_dim.167) | data formatting | bytes 16384 | tf_op jit(solution)/shard_map/jit(_where)/broadcast_in_dim | solution.py:38
  93.5 2.0 broadcast_in_dim.174
  95.5 3.2 %broadcast_in_dim.175 = pred[32,256]{1,0:T(8,128)(4,1)} reshape(pred[256,4,4,2]{3,2,1,0:T(4,128)(4,1)} %broadcast_in_dim.174) | data formatting | bytes 16384 | tf_op jit(solution)/shard_map/jit(_where)/broadcast_in_dim | solution.py:38
  99.9 2.6 broadcast_in_dim.146
  102.5 39.7 %all_gather.13 = bf16[512,5,128]{2,0,1:T(8,128)(2,1)} all-gather(bf16[32,5,128]{2,0,1:T(8,128)(2,1)S(1)} %constant_dynamic-slice_fusion), channel_id=1, replica_groups=mesh['flux'=16,'obs'=32] {'flux'}, dimensions={0}, use_global_device_ids=true | all-gather | bytes 696320 | tf_op jit(solution)/shard_map/all_gather | solution.py:22
  142.3 2.2 copy.159
  144.4 2.2 fusion.4
  152.5 2.2 broadcast_in_dim.157
  159.2 8.6 %multiply_reduce_fusion.5 = f32[32,256]{1,0:T(8,128)S(1)} fusion(f32[32,256,128]{2,1,0:T(8,128)S(1)} %bitcast.81, f32[32,256,128]{2,1,0:T(8,128)S(1)} %bitcast.80, f32[32,256,128]{2,1,0:T(8,128)S(1)} %bitcast.79, f32[32,256,128]{2,1,0:T(8,128)S(1)} %bitcast.78, f32[32,256,128]{2,1,0:T(8,128)S(1)} %bitcast.82, pred[32,256]{1,0:T(8,128)(4,1)S(1)} %copy-done.7, ...), kind=kLoop, calls=%fused_computation.5 | loop fusion | flops 12574720 | bytes 23142400 | tf_op jit(solution)/shard_map/reduce_sum | solution.py:41
  167.8 4.0 %reduce_sum.81 = f32[256,4,4,2]{3,2,1,0:T(4,128)} reshape(f32[32,256]{1,0:T(8,128)S(1)} %multiply_reduce_fusion.5) | data formatting | bytes 65536 | tf_op jit(solution)/shard_map/reduce_sum | solution.py:41
  171.9 2.1 reduce_sum.82
  174.0 22.4 %all-gather = f32[8192,4]{0,1:T(4,128)S(1)} all-gather(f32[256,4]{0,1:T(4,128)S(1)} %copy.171), channel_id=2, replica_groups=mesh['flux'=16,'obs'=32] {'obs'}, dimensions={0}, use_global_device_ids=true | all-gather | bytes 135168 | tf_op jit(solution)/shard_map/all_gather | solution.py:42
  202.4 18.6 %multiply_reduce_fusion = (f32[256,4,128]{2,1,0:T(4,128)}, f32[256,4,128]{2,1,0:T(4,128)}, f32[256,4,128]{2,1,0:T(4,128)}, f32[256,4,128]{2,1,0:T(4,128)}, f32[256,4,128]{2,1,0:T(4,128)}) fusion(f32[256,4,2]{2,1,0:T(4,128)} %copy.178, f32[256,4,2]{2,1,0:T(4,128)} %copy.177, f32[256,4,2]{2,1,0:T(4,128)} %copy.176, f32[256,4,2]{2,1,0:T(4,128)} %copy.175, ...), kind=kLoop, calls=%fused_computation | loop fusion | flops 10878976 | bytes 4759552 | tf_op jit(solution)/shard_map/reduce_sum | solution.py:49
  221.0 10.5 %stack.23 = f32[256,4,5,128]{3,2,1,0:T(8,128)} concatenate(f32[256,4,1,128]{3,2,1,0:T(1,128)} %bitcast.91, f32[256,4,1,128]{3,2,1,0:T(1,128)} %bitcast.90, f32[256,4,1,128]{3,2,1,0:T(1,128)} %bitcast.89, f32[256,4,1,128]{3,2,1,0:T(1,128)} %bitcast.88, f32[256,4,1,128]{3,2,1,0:T(1,128)} %bitcast.87), dimensions={2} | concatenate | bytes 5242880 | tf_op jit(solution)/shard_map/stack | solution.py:51
  231.5 3.5 %fusion.1 = f32[512,640]{1,0:T(8,128)S(1)} fusion(f32[128,8,5,128]{3,2,1,0:T(8,128)} %bitcast.85, s32[1024]{0:T(1024)S(1)} %copy-done.9), kind=kOutput, calls=%fused_computation.10 | convolution fusion | flops 674234368 | bytes 3936256 | tf_op jit(solution)/shard_map/dot_general | solution.py:57
  235.0 4.4 %fusion.6 = f32[512,640]{1,0:T(8,128)} fusion(f32[512,640]{1,0:T(8,128)S(1)} %fusion.1, f32[128,8,5,128]{3,2,1,0:T(8,128)} %bitcast.86, s32[1024]{0:T(1024)S(1)} %copy-done.9), kind=kOutput, calls=%fused_computation.15 | convolution fusion | flops 671940608 | bytes 5246976 | tf_op jit(solution)/shard_map/dot_general | solution.py:55
  239.4 1.7 copy.179
  241.1 1.8 copy.180
  243.6 67.7 %reduce-scatter.2.cloned.1.call-done = f32[32,5,128]{2,1,0:T(8,128)} async-done(((f32[512,5,128]{2,1,0:T(8,128)}), f32[32,5,128]{2,1,0:T(8,128)}) %reduce-scatter.2.cloned.1.call-update) | async-done | bytes 81936 | tf_op jit(solution)/shard_map/reduce_scatter | solution.py:58
  (73 shorter events, 26.7 us)
Async XLA Ops:
  7.2 95.3 %copy-start = (bf16[32,5,4096]{2,0,1:T(8,128)(2,1)S(1)}, bf16[32,5,4096]{2,0,1:T(8,128)(2,1)}, u32[]{:S(2)}) copy-start(bf16[32,5,4096]{2,0,1:T(8,128)(2,1)} %param.11) | copy-start | bytes 3932164
  10.6 11.8 %copy-start.12 = (s32[8,4]{0,1:T(4,128)S(1)}, s32[8,4]{0,1:T(4,128)}, u32[]{:S(2)}) copy-start(s32[8,4]{0,1:T(4,128)} %param.8) | copy-start | bytes 388
  10.6 11.8 %copy-start.10 = (s32[512]{0:T(512)S(1)}, s32[512]{0:T(512)}, u32[]{:S(2)}) copy-start(s32[512]{0:T(512)} %param.10) | copy-start | bytes 6148
  10.6 11.8 %copy-start.11 = (s32[8,4]{0,1:T(4,128)S(1)}, s32[8,4]{0,1:T(4,128)}, u32[]{:S(2)}) copy-start(s32[8,4]{0,1:T(4,128)} %param.9) | copy-start | bytes 388
  10.7 12.1 %copy-start.13 = (f32[8,4]{0,1:T(4,128)S(1)}, f32[8,4]{0,1:T(4,128)}, u32[]{:S(2)}) copy-start(f32[8,4]{0,1:T(4,128)} %param.13) | copy-start | bytes 388
  10.7 12.1 %copy-start.14 = (f32[8,4]{0,1:T(4,128)S(1)}, f32[8,4]{0,1:T(4,128)}, u32[]{:S(2)}) copy-start(f32[8,4]{0,1:T(4,128)} %param.12) | copy-start | bytes 388
  12.8 139.7 %all-to-all-start = ((bf16[32,256,128]{2,1,0:T(8,128)(2,1)}), bf16[32,256,128]{2,1,0:T(8,128)(2,1)S(1)}, u32[]{:S(2)}, u32[]{:S(2)}) async-start(bf16[32,256,128]{2,1,0:T(8,128)(2,1)} %copy.154), calls=%async_computation | async-start | bytes 4194304 | tf_op jit(solution)/shard_map/all_to_all | solution.py:25
  22.4 289.0 %reduce-scatter.2.cloned.1.call-start = ((), (), s32[]{:S(2)}) async-start(), calls=%async_computation.2 | async-start | bytes 2228224 | tf_op jit(solution)/shard_map/reduce_scatter | solution.py:58
  152.5 2.2 copy-start.4
  152.5 3.3 %copy-start.3 = (f32[256,4,128]{2,1,0:T(4,128)S(1)}, f32[256,4,128]{2,1,0:T(4,128)}, u32[]{:S(2)}) copy-start(f32[256,4,128]{2,1,0:T(4,128)} %copy.166) | copy-start | bytes 1572868
  154.8 2.2 copy-start.2
  155.9 2.2 copy-start.1
  157.0 2.2 copy-start.5
  157.0 2.2 copy-start.6
  157.0 2.2 copy-start.7
  167.8 28.6 %copy-start.8 = (f32[256,4]{0,1:T(4,128)S(1)}, f32[256,4]{0,1:T(4,128)}, u32[]{:S(2)}) copy-start(f32[256,4]{0,1:T(4,128)} %copy.185) | copy-start | bytes 12292
  221.0 10.5 %copy-start.9 = (s32[1024]{0:T(1024)S(1)}, s32[1024]{0:T(1024)}, u32[]{:S(2)}) copy-start(s32[1024]{0:T(1024)} %eq.73) | copy-start | bytes 12292
Sparse Core Ops, SparseCore 0:
  243.1 68.2 reduce-scatter.1
